TPU v7x, 32 devices: a whole 2x2x4 slice. The times are simulated.
32 devices in a mesh: dp: 8 (over y, x, core), tensor: 4 (over z).
Axes of the slice: x: 2, y: 2, z: 4, core: 2. Of those that a mesh axis runs over, the one named last changes fastest.
Arguments:
- teacher_input: bfloat16 [8, 1024, 1280], P('dp', 'tensor'), may hold values from -6 to 6
- teacher_upstream: bfloat16 [8, 1024, 1280], P('dp', 'tensor'), may hold values from -6 to 6
- teacher_attn_gain: bfloat16 [1280], P('dp'), may hold values from 0.25 to 1.75
- teacher_attn_shift: bfloat16 [1280], P('dp'), may hold values from -1.75 to 1.75
- teacher_qkv_weight: bfloat16 [3, 1280, 1536], P(None, 'dp', 'tensor'), may hold values from -0.15625 to 0.15625
- teacher_qv_bias: bfloat16 [2, 1536], P(None, 'tensor'), may hold values from -0.625 to 0.625
- teacher_out_weight: bfloat16 [1536, 1280], P('tensor', 'dp'), may hold values from -1.25 to 1.25
- teacher_out_bias: bfloat16 [1280], P('dp'), may hold values from -1.75 to 1.75
- teacher_mlp_gain: bfloat16 [1280], P('dp'), may hold values from 0.25 to 1.75
- teacher_mlp_shift: bfloat16 [1280], P('dp'), may hold values from -1.75 to 1.75
- teacher_fc_weight: bfloat16 [1280, 5120], P('dp', 'tensor'), may hold values from -0.15625 to 0.15625
- teacher_fc_bias: bfloat16 [5120], P('tensor'), may hold values from -1.75 to 1.75
- teacher_proj_weight: bfloat16 [5120, 1280], P('tensor', 'dp'), may hold values from -0.078125 to 0.078125
- teacher_proj_bias: bfloat16 [1280], P('dp'), may hold values from -1.75 to 1.75
- student_input: bfloat16 [8, 1024, 768], P('dp', 'tensor'), may hold values from -6 to 6
- student_upstream: bfloat16 [8, 1024, 768], P('dp', 'tensor'), may hold values from -6 to 6
- student_attn_gain: bfloat16 [768], P('dp'), may hold values from 0.25 to 1.75
- student_attn_shift: bfloat16 [768], P('dp'), may hold values from -1.75 to 1.75
- student_qkv_weight: bfloat16 [3, 768, 768], P(None, 'dp', 'tensor'), may hold values from -0.21875 to 0.21875
- student_qv_bias: bfloat16 [2, 768], P(None, 'tensor'), may hold values from -0.625 to 0.625
- student_out_weight: bfloat16 [768, 768], P('tensor', 'dp'), may hold values from -1.75 to 1.75
- student_out_bias: bfloat16 [768], P('dp'), may hold values from -1.75 to 1.75
- student_mlp_gain: bfloat16 [768], P('dp'), may hold values from 0.25 to 1.75
- student_mlp_shift: bfloat16 [768], P('dp'), may hold values from -1.75 to 1.75
- student_fc_weight: bfloat16 [768, 3072], P('dp', 'tensor'), may hold values from -0.21875 to 0.21875
- student_fc_bias: bfloat16 [3072], P('tensor'), may hold values from -1.75 to 1.75
- student_proj_weight: bfloat16 [3072, 768], P('tensor', 'dp'), may hold values from -0.109375 to 0.109375
- student_proj_bias: bfloat16 [768], P('dp'), may hold values from -1.75 to 1.75
- span_starts: int32 [8], P('dp'), may hold values from 0 to 768, as said below
- head_slots: int32 [24], P('tensor'), may hold values from 0 to 1, as said below
Outputs:
- teacher_output: bfloat16 [8, 1024, 1280], P('dp', 'tensor')
- teacher_input_grad: bfloat16 [8, 1024, 1280], P('dp', 'tensor')
- teacher_attn_gain_grad: float32 [1280], P('dp')
- teacher_attn_shift_grad: float32 [1280], P('dp')
- teacher_qkv_weight_grad: float32 [3, 1280, 1536], P(None, 'dp', 'tensor')
- teacher_qv_bias_grad: float32 [2, 1536], P(None, 'tensor')
- teacher_out_weight_grad: float32 [1536, 1280], P('tensor', 'dp')
- teacher_out_bias_grad: float32 [1280], P('dp')
- teacher_mlp_gain_grad: float32 [1280], P('dp')
- teacher_mlp_shift_grad: float32 [1280], P('dp')
- teacher_fc_weight_grad: float32 [1280, 5120], P('dp', 'tensor')
- teacher_fc_bias_grad: float32 [5120], P('tensor')
- teacher_proj_weight_grad: float32 [5120, 1280], P('tensor', 'dp')
- teacher_proj_bias_grad: float32 [1280], P('dp')
- student_output: bfloat16 [8, 1024, 768], P('dp', 'tensor')
- student_input_grad: bfloat16 [8, 1024, 768], P('dp', 'tensor')
- student_attn_gain_grad: float32 [768], P('dp')
- student_attn_shift_grad: float32 [768], P('dp')
- student_qkv_weight_grad: float32 [3, 768, 768], P(None, 'dp', 'tensor')
- student_qv_bias_grad: float32 [2, 768], P(None, 'tensor')
- student_out_weight_grad: float32 [768, 768], P('tensor', 'dp')
- student_out_bias_grad: float32 [768], P('dp')
- student_mlp_gain_grad: float32 [768], P('dp')
- student_mlp_shift_grad: float32 [768], P('dp')
- student_fc_weight_grad: float32 [768, 3072], P('dp', 'tensor')
- student_fc_bias_grad: float32 [3072], P('tensor')
- student_proj_weight_grad: float32 [3072, 768], P('tensor', 'dp')
- student_proj_bias_grad: float32 [768], P('dp')
Inputs may be any that keep to these rules, and one draw needn't show every extreme that they name: `span_starts`: some sequence starts its span at 0 and some at 768. `head_slots`: exactly 20 of the 24 slots are 1.
All inputs are finite; a program needn't handle non-finite values.
Results may differ from a plain program's by a relative error of at most 0.02.
Values may be sent and summed in bfloat16 or wider, within the bound.
No kernel may reach another device: no remote copies, remote signals or barrier semaphores. Data moves between devices by JAX's collectives and lax.ppermute only.
A program may use at most 256 MiB of HBM per device.

v0:
```python
import jax
import jax.numpy as jnp
from jax import lax
from jax.sharding import PartitionSpec as P

HD = 64
SPAN = 256
epsilon = 1e-05
negative = -1e30


def layer_norm(values, norm_gain, norm_shift):
    center = values - jnp.mean(values, axis=-1, keepdims=True)
    spread = jnp.mean(center * center, axis=-1, keepdims=True)
    return center * lax.rsqrt(spread + epsilon) * norm_gain + norm_shift


def gelu_tanh(values):
    return jax.nn.gelu(values, approximate=True)


def visibility(first_row, block_rows, length, span_start):
    query_pos = first_row + jnp.arange(block_rows, dtype=jnp.int32)
    key_pos = jnp.arange(length, dtype=jnp.int32)
    query_in = (query_pos >= span_start) & (query_pos < span_start + SPAN)
    key_in = (key_pos >= span_start) & (key_pos < span_start + SPAN)
    return (key_pos[None, :] <= query_pos[:, None]) | query_in[:, None] & key_in[None, :]


def block_scores(query_block, key_rows, visible, score_scale):
    scores = (
        jnp.einsum("qhe,khe->hqk", query_block, key_rows, preferred_element_type=jnp.float32)
        * score_scale
    )
    return jnp.where(visible[None], scores, negative)


def attention_forward(query_rows, key_rows, value_rows, span_start, block_rows, score_scale):
    length = query_rows.shape[0]
    results = []
    log_sums = []
    for block_index in range(length // block_rows):
        first_row = block_index * block_rows
        visible = visibility(first_row, block_rows, length, span_start)
        scores = block_scores(
            query_rows[first_row : first_row + block_rows], key_rows, visible, score_scale
        )
        row_peak = jnp.max(scores, axis=-1, keepdims=True)
        raised = jnp.exp(scores - row_peak)
        row_total = jnp.sum(raised, axis=-1, keepdims=True)
        weights = (raised / row_total).astype(jnp.bfloat16)
        results.append(
            jnp.einsum("hqk,khe->qhe", weights, value_rows, preferred_element_type=jnp.float32)
        )
        log_sums.append(row_peak + jnp.log(row_total))
    return (jnp.concatenate(results, axis=0), log_sums)


def attention_backward(
    query_rows, key_rows, value_rows, log_sums, heads_grad, span_start, block_rows, score_scale
):
    length = query_rows.shape[0]
    query_grads = []
    key_grad = jnp.zeros(key_rows.shape, jnp.float32)
    value_grad = jnp.zeros(value_rows.shape, jnp.float32)
    for block_index in range(length // block_rows):
        first_row = block_index * block_rows
        last_row = first_row + block_rows
        visible = visibility(first_row, block_rows, length, span_start)
        scores = block_scores(query_rows[first_row:last_row], key_rows, visible, score_scale)
        probability = jnp.exp(scores - log_sums[block_index])
        grad_block = heads_grad[first_row:last_row]
        value_grad = value_grad + jnp.einsum(
            "hqk,qhe->khe",
            probability.astype(jnp.bfloat16),
            grad_block,
            preferred_element_type=jnp.float32,
        )
        prob_grad = jnp.einsum(
            "qhe,khe->hqk", grad_block, value_rows, preferred_element_type=jnp.float32
        )
        weighted = jnp.sum(probability * prob_grad, axis=-1, keepdims=True)
        score_grad = (probability * (prob_grad - weighted)).astype(jnp.bfloat16)
        query_grads.append(
            jnp.einsum("hqk,khe->qhe", score_grad, key_rows, preferred_element_type=jnp.float32)
            * score_scale
        )
        key_grad = (
            key_grad
            + jnp.einsum(
                "hqk,qhe->khe",
                score_grad,
                query_rows[first_row:last_row],
                preferred_element_type=jnp.float32,
            )
            * score_scale
        )
    return (jnp.concatenate(query_grads, axis=0), key_grad, value_grad)


def gather_rows(normed):
    return lax.all_gather(normed, "tensor", axis=0, tiled=True)


def gather_grads(branch_grad):
    return lax.all_gather(branch_grad, "tensor", axis=0, tiled=True)


def sum_rows(left_rows, right_weight):
    return lax.psum_scatter(
        jnp.dot(left_rows, right_weight, preferred_element_type=jnp.float32).astype(jnp.bfloat16),
        "tensor",
        scatter_dimension=0,
        tiled=True,
    ).astype(jnp.float32)


def back_rows(grad_stack, weight_stack):
    return lax.psum_scatter(
        jnp.einsum(
            "sle,sde->ld", grad_stack, weight_stack, preferred_element_type=jnp.float32
        ).astype(jnp.bfloat16),
        "tensor",
        scatter_dimension=0,
        tiled=True,
    ).astype(jnp.float32)


def run_block(
    inputs,
    upstream,
    attn_gain,
    attn_shift,
    qkv_weight,
    qv_bias,
    out_weight,
    out_bias,
    mlp_gain,
    mlp_shift,
    fc_weight,
    fc_bias,
    proj_weight,
    proj_bias,
    span_start,
    head_keep,
):
    gathered = (
        lax.all_gather(qkv_weight, "dp", axis=1, tiled=True),
        lax.all_gather(out_weight, "dp", axis=1, tiled=True),
        lax.all_gather(fc_weight, "dp", axis=0, tiled=True),
        lax.all_gather(proj_weight, "dp", axis=1, tiled=True),
        lax.all_gather(attn_gain, "dp", axis=0, tiled=True),
        lax.all_gather(attn_shift, "dp", axis=0, tiled=True),
        lax.all_gather(out_bias, "dp", axis=0, tiled=True),
        lax.all_gather(mlp_gain, "dp", axis=0, tiled=True),
        lax.all_gather(mlp_shift, "dp", axis=0, tiled=True),
        lax.all_gather(proj_bias, "dp", axis=0, tiled=True),
    )
    qkv_full, out_full, fc_full, proj_full = (gathered[0], gathered[1], gathered[2], gathered[3])
    gain_one = gathered[4].astype(jnp.float32)
    shift_one = gathered[5].astype(jnp.float32)
    bias_out = gathered[6].astype(jnp.float32)
    gain_two = gathered[7].astype(jnp.float32)
    shift_two = gathered[8].astype(jnp.float32)
    bias_proj = gathered[9].astype(jnp.float32)
    rows_first = inputs[0].astype(jnp.float32)
    normed, norm_back_one = jax.vjp(layer_norm, rows_first, gain_one, shift_one)
    normed_all = gather_rows(normed.astype(jnp.bfloat16))
    projected = jnp.einsum("ld,tde->tle", normed_all, qkv_full, preferred_element_type=jnp.float32)
    bias_pair = qv_bias.astype(jnp.float32)
    length = normed_all.shape[0]
    head_count = head_keep.shape[0]
    head_split = (length, head_count, HD)
    query_rows = (projected[0] + bias_pair[0]).astype(jnp.bfloat16).reshape(head_split)
    key_rows = projected[1].astype(jnp.bfloat16).reshape(head_split)
    value_rows = (projected[2] + bias_pair[1]).astype(jnp.bfloat16).reshape(head_split)
    block_rows = min(512, length)
    score_scale = 1.0 / HD**0.5
    attended, log_sums = attention_forward(
        query_rows, key_rows, value_rows, span_start, block_rows, score_scale
    )
    keep_float = head_keep.astype(jnp.float32)[None, :, None]
    heads_low = (attended * keep_float).astype(jnp.bfloat16).reshape(length, head_count * HD)
    attn_sum = sum_rows(heads_low, out_full)
    middle = rows_first + (attn_sum + bias_out)
    normed_two, norm_back_two = jax.vjp(layer_norm, middle, gain_two, shift_two)
    normed_two_all = gather_rows(normed_two.astype(jnp.bfloat16))
    hidden_pre = jnp.dot(
        normed_two_all, fc_full, preferred_element_type=jnp.float32
    ) + fc_bias.astype(jnp.float32)
    hidden, gelu_back = jax.vjp(gelu_tanh, hidden_pre)
    hidden_low = hidden.astype(jnp.bfloat16)
    mlp_sum = sum_rows(hidden_low, proj_full)
    result = middle + (mlp_sum + bias_proj)
    outputs = result.astype(jnp.bfloat16)[None]
    grad_result = upstream[0].astype(jnp.float32)
    grad_mlp_all = gather_grads(upstream[0])
    proj_bias_grad = jnp.sum(grad_mlp_all, axis=0, dtype=jnp.float32)
    proj_grad = jnp.einsum(
        "lf,ld->fd", hidden_low, grad_mlp_all, preferred_element_type=jnp.float32
    )
    hidden_grad = jnp.einsum(
        "ld,fd->lf", grad_mlp_all, proj_full, preferred_element_type=jnp.float32
    )
    pre_grad = gelu_back(hidden_grad)[0].astype(jnp.bfloat16)
    fc_bias_grad = jnp.sum(pre_grad, axis=0, dtype=jnp.float32)
    fc_grad = jnp.einsum("ld,lf->df", normed_two_all, pre_grad, preferred_element_type=jnp.float32)
    normed_two_grad = back_rows(pre_grad[None], fc_full[None])
    middle_from_norm, gain_two_grad, shift_two_grad = norm_back_two(normed_two_grad)
    middle_grad = grad_result + middle_from_norm
    grad_attn_all = gather_grads(middle_grad.astype(jnp.bfloat16))
    out_bias_grad = jnp.sum(grad_attn_all, axis=0, dtype=jnp.float32)
    out_grad = jnp.einsum("le,ld->ed", heads_low, grad_attn_all, preferred_element_type=jnp.float32)
    heads_grad = (
        jnp.einsum("ld,ed->le", grad_attn_all, out_full, preferred_element_type=jnp.float32)
        .astype(jnp.bfloat16)
        .reshape(head_split)
    )
    heads_grad = heads_grad * head_keep.astype(jnp.bfloat16)[None, :, None]
    query_grad, key_grad, value_grad = attention_backward(
        query_rows, key_rows, value_rows, log_sums, heads_grad, span_start, block_rows, score_scale
    )
    qkv_low = jnp.stack(
        [
            query_grad.reshape(length, head_count * HD),
            key_grad.reshape(length, head_count * HD),
            value_grad.reshape(length, head_count * HD),
        ]
    ).astype(jnp.bfloat16)
    qv_bias_grad = jnp.stack(
        [
            jnp.sum(qkv_low[0], axis=0, dtype=jnp.float32),
            jnp.sum(qkv_low[2], axis=0, dtype=jnp.float32),
        ]
    )
    qkv_grad = jnp.einsum("ld,tle->tde", normed_all, qkv_low, preferred_element_type=jnp.float32)
    normed_grad = back_rows(qkv_low, qkv_full)
    rows_from_norm, gain_one_grad, shift_one_grad = norm_back_one(normed_grad)
    input_grad = (middle_grad + rows_from_norm).astype(jnp.bfloat16)[None]
    norm_sums = lax.psum((gain_one_grad, shift_one_grad, gain_two_grad, shift_two_grad), "tensor")
    matrices = (
        qkv_grad,
        out_grad,
        fc_grad,
        proj_grad,
        norm_sums[0],
        norm_sums[1],
        out_bias_grad,
        norm_sums[2],
        norm_sums[3],
        proj_bias_grad,
    )
    biases = (qv_bias_grad, fc_bias_grad)
    return (outputs, input_grad, matrices, biases)


def arrange(outputs, input_grad, matrices, biases):
    return (
        outputs,
        input_grad,
        matrices[4],
        matrices[5],
        matrices[0],
        biases[0],
        matrices[1],
        matrices[6],
        matrices[7],
        matrices[8],
        matrices[2],
        biases[1],
        matrices[3],
        matrices[9],
    )


def on_device(
    teacher_input,
    teacher_upstream,
    teacher_attn_gain,
    teacher_attn_shift,
    teacher_qkv_weight,
    teacher_qv_bias,
    teacher_out_weight,
    teacher_out_bias,
    teacher_mlp_gain,
    teacher_mlp_shift,
    teacher_fc_weight,
    teacher_fc_bias,
    teacher_proj_weight,
    teacher_proj_bias,
    student_input,
    student_upstream,
    student_attn_gain,
    student_attn_shift,
    student_qkv_weight,
    student_qv_bias,
    student_out_weight,
    student_out_bias,
    student_mlp_gain,
    student_mlp_shift,
    student_fc_weight,
    student_fc_bias,
    student_proj_weight,
    student_proj_bias,
    span_starts,
    head_slots,
):
    span_start = span_starts[0]
    teacher = run_block(
        teacher_input,
        teacher_upstream,
        teacher_attn_gain,
        teacher_attn_shift,
        teacher_qkv_weight,
        teacher_qv_bias,
        teacher_out_weight,
        teacher_out_bias,
        teacher_mlp_gain,
        teacher_mlp_shift,
        teacher_fc_weight,
        teacher_fc_bias,
        teacher_proj_weight,
        teacher_proj_bias,
        span_start,
        head_slots,
    )
    student_keep = jnp.ones((student_qv_bias.shape[1] // HD,), jnp.int32)
    student = run_block(
        student_input,
        student_upstream,
        student_attn_gain,
        student_attn_shift,
        student_qkv_weight,
        student_qv_bias,
        student_out_weight,
        student_out_bias,
        student_mlp_gain,
        student_mlp_shift,
        student_fc_weight,
        student_fc_bias,
        student_proj_weight,
        student_proj_bias,
        span_start,
        student_keep,
    )
    teach_parts = teacher[2]
    learn_parts = student[2]
    summed = (
        lax.psum_scatter(teach_parts[0], "dp", scatter_dimension=1, tiled=True),
        lax.psum_scatter(teach_parts[1], "dp", scatter_dimension=1, tiled=True),
        lax.psum_scatter(teach_parts[2], "dp", scatter_dimension=0, tiled=True),
        lax.psum_scatter(teach_parts[3], "dp", scatter_dimension=1, tiled=True),
        lax.psum_scatter(teach_parts[4], "dp", scatter_dimension=0, tiled=True),
        lax.psum_scatter(teach_parts[5], "dp", scatter_dimension=0, tiled=True),
        lax.psum_scatter(teach_parts[6], "dp", scatter_dimension=0, tiled=True),
        lax.psum_scatter(teach_parts[7], "dp", scatter_dimension=0, tiled=True),
        lax.psum_scatter(teach_parts[8], "dp", scatter_dimension=0, tiled=True),
        lax.psum_scatter(teach_parts[9], "dp", scatter_dimension=0, tiled=True),
        lax.psum_scatter(learn_parts[0], "dp", scatter_dimension=1, tiled=True),
        lax.psum_scatter(learn_parts[1], "dp", scatter_dimension=1, tiled=True),
        lax.psum_scatter(learn_parts[2], "dp", scatter_dimension=0, tiled=True),
        lax.psum_scatter(learn_parts[3], "dp", scatter_dimension=1, tiled=True),
        lax.psum_scatter(learn_parts[4], "dp", scatter_dimension=0, tiled=True),
        lax.psum_scatter(learn_parts[5], "dp", scatter_dimension=0, tiled=True),
        lax.psum_scatter(learn_parts[6], "dp", scatter_dimension=0, tiled=True),
        lax.psum_scatter(learn_parts[7], "dp", scatter_dimension=0, tiled=True),
        lax.psum_scatter(learn_parts[8], "dp", scatter_dimension=0, tiled=True),
        lax.psum_scatter(learn_parts[9], "dp", scatter_dimension=0, tiled=True),
    )
    totals = lax.psum((teacher[3][0], teacher[3][1], student[3][0], student[3][1]), "dp")
    teacher_matrices = summed[0:10]
    student_matrices = summed[10:20]
    teacher_biases = (totals[0], totals[1])
    student_biases = (totals[2], totals[3])
    return arrange(teacher[0], teacher[1], teacher_matrices, teacher_biases) + arrange(
        student[0], student[1], student_matrices, student_biases
    )


def solution(mesh):
    in_specs = (
        P("dp", "tensor", None),
        P("dp", "tensor", None),
        P("dp"),
        P("dp"),
        P(None, "dp", "tensor"),
        P(None, "tensor"),
        P("tensor", "dp"),
        P("dp"),
        P("dp"),
        P("dp"),
        P("dp", "tensor"),
        P("tensor"),
        P("tensor", "dp"),
        P("dp"),
        P("dp", "tensor", None),
        P("dp", "tensor", None),
        P("dp"),
        P("dp"),
        P(None, "dp", "tensor"),
        P(None, "tensor"),
        P("tensor", "dp"),
        P("dp"),
        P("dp"),
        P("dp"),
        P("dp", "tensor"),
        P("tensor"),
        P("tensor", "dp"),
        P("dp"),
        P("dp"),
        P("tensor"),
    )
    out_specs = (
        P("dp", "tensor", None),
        P("dp", "tensor", None),
        P("dp"),
        P("dp"),
        P(None, "dp", "tensor"),
        P(None, "tensor"),
        P("tensor", "dp"),
        P("dp"),
        P("dp"),
        P("dp"),
        P("dp", "tensor"),
        P("tensor"),
        P("tensor", "dp"),
        P("dp"),
        P("dp", "tensor", None),
        P("dp", "tensor", None),
        P("dp"),
        P("dp"),
        P(None, "dp", "tensor"),
        P(None, "tensor"),
        P("tensor", "dp"),
        P("dp"),
        P("dp"),
        P("dp"),
        P("dp", "tensor"),
        P("tensor"),
        P("tensor", "dp"),
        P("dp"),
    )
    return jax.shard_map(
        on_device, mesh=mesh, in_specs=in_specs, out_specs=out_specs, check_vma=False
    )
```

profile of v0, /device:TPU:0, one launch (start us, length us, event | category | flops | bytes accessed | tf_op | source)
XLA Modules:
  0.0 1425.0 jit_solution(5786993439719821327)
XLA Ops:
  22.5 26.5 %all-reduce.27 = (bf16[1280]{0:T(1024)(128)(2,1)}, bf16[1280]{0:T(1024)(128)(2,1)}, bf16[1280]{0:T(1024)(128)(2,1)S(1)}, bf16[1280]{0:T(1024)(128)(2,1)S(1)}, bf...) all-reduce(bf16[1280]{0:T(1024)(128)(2,1)S(1)} %dynamic-update-slic, ...), channel_id=1, replica_groups=mesh['dp'=8,'tensor'=4] {'dp'}, use_global_device_ids=true, to_apply=%add.4 | all-reduce | flops 12288 | bytes 49152
  56.3 10.9 all_gather.88
  67.2 13.4 all_gather.101
  108.0 35.6 %all-gather.16.cloned.1.call-done = bf16[1024,1280]{1,0:T(8,128)(2,1)} async-done(((bf16[256,1280]{1,0:T(8,128)(2,1)}), bf16[1024,1280]{1,0:T(8,128)(2,1)}) %all-gather.16.cloned.1.call-update) | async-done | bytes 2621456 | tf_op jit(solution)/shard_map/all_gather | solution.py:102
  143.6 32.2 %all-gather.18.cloned.1.call-done = bf16[3,1280,384]{2,1,0:T(8,128)(2,1)} async-done(((bf16[3,160,384]{2,1,0:T(8,128)(2,1)}), bf16[3,1280,384]{2,1,0:T(8,128)(2,1)}) %all-gather.18.cloned.1.call-update) | async-done | bytes 2949136 | tf_op jit(solution)/shard_map/all_gather | solution.py:148
  220.0 46.6 %reduce-scatter.20.cloned.1.call-done = bf16[256,1280]{1,0:T(8,128)(2,1)} async-done(((bf16[1024,1280]{1,0:T(8,128)(2,1)}), bf16[256,1280]{1,0:T(8,128)(2,1)}) %reduce-scatter.20.cloned.1.call-update) | async-done | bytes 655376 | tf_op jit(solution)/shard_map/reduce_scatter | solution.py:110
  273.4 18.7 %all-gather.32.cloned.1.call-done = bf16[768,768]{1,0:T(8,128)(2,1)} async-done(((bf16[96,768]{1,0:T(8,128)(2,1)}), bf16[768,768]{1,0:T(8,128)(2,1)}) %all-gather.32.cloned.1.call-update) | async-done | bytes 1179664 | tf_op jit(solution)/shard_map/all_gather | solution.py:150
  292.1 39.3 %all-gather.30.cloned.1.call-done = bf16[1024,768]{1,0:T(8,128)(2,1)} async-done(((bf16[256,768]{1,0:T(8,128)(2,1)}), bf16[1024,768]{1,0:T(8,128)(2,1)}) %all-gather.30.cloned.1.call-update) | async-done | bytes 1572880 | tf_op jit(solution)/shard_map/all_gather | solution.py:102
  336.2 20.0 %all-gather.34.cloned.1.call-done = bf16[768,768]{0,1:T(8,128)(2,1)} async-done(((bf16[768,96]{0,1:T(8,128)(2,1)}), bf16[768,768]{0,1:T(8,128)(2,1)}) %all-gather.34.cloned.1.call-update) | async-done | bytes 1179664 | tf_op jit(solution)/shard_map/all_gather | solution.py:151
  356.2 38.7 %all-gather.40.cloned.1.call-done = bf16[1,1024,768]{2,1,0:T(8,128)(2,1)} async-done(((bf16[1,256,768]{2,1,0:T(8,128)(2,1)}), bf16[1,1024,768]{2,1,0:T(8,128)(2,1)}) %all-gather.40.cloned.1.call-update) | async-done | bytes 1572880 | tf_op jit(solution)/shard_map/all_gather | solution.py:106
  411.0 17.4 %all-gather.22.cloned.1.call-done = bf16[1280,1280]{1,0:T(8,128)(2,1)} async-done(((bf16[160,1280]{1,0:T(8,128)(2,1)}), bf16[1280,1280]{1,0:T(8,128)(2,1)}) %all-gather.22.cloned.1.call-update) | async-done | bytes 3276816 | tf_op jit(solution)/shard_map/all_gather | solution.py:150
  428.4 57.0 %all-gather.20.cloned.1.call-done = bf16[1024,1280]{1,0:T(8,128)(2,1)} async-done(((bf16[256,1280]{1,0:T(8,128)(2,1)}), bf16[1024,1280]{1,0:T(8,128)(2,1)}) %all-gather.20.cloned.1.call-update) | async-done | bytes 2621456 | tf_op jit(solution)/shard_map/all_gather | solution.py:102
  493.9 46.5 %all-gather.38.cloned.1.call-done = bf16[1,1024,1280]{2,1,0:T(8,128)(2,1)} async-done(((bf16[1,256,1280]{2,1,0:T(8,128)(2,1)}), bf16[1,1024,1280]{2,1,0:T(8,128)(2,1)}) %all-gather.38.cloned.1.call-update) | async-done | bytes 2621456 | tf_op jit(solution)/shard_map/all_gather | solution.py:106
  540.4 33.6 %all-gather.24.cloned.1.call-done = bf16[1280,1280]{0,1:T(8,128)(2,1)} async-done(((bf16[1280,160]{0,1:T(8,128)(2,1)}), bf16[1280,1280]{0,1:T(8,128)(2,1)}) %all-gather.24.cloned.1.call-update) | async-done | bytes 3276816 | tf_op jit(solution)/shard_map/all_gather | solution.py:151
  574.0 10.7 convert_reduce_fusion.1
  591.2 9.7 convolution_convert_fusion.2
  601.0 10.4 reduce-scatter.38.cloned.1.call-done
  613.5 34.4 %reduce-scatter.36.cloned.1.call-done = bf16[256,768]{1,0:T(8,128)(2,1)} async-done(((bf16[1024,768]{1,0:T(8,128)(2,1)}), bf16[256,768]{1,0:T(8,128)(2,1)}) %reduce-scatter.36.cloned.1.call-update) | async-done | bytes 393232 | tf_op jit(solution)/shard_map/reduce_scatter | solution.py:110
  652.7 48.5 %reduce-scatter.24.cloned.1.call-done = bf16[256,1280]{1,0:T(8,128)(2,1)} async-done(((bf16[1024,1280]{1,0:T(8,128)(2,1)}), bf16[256,1280]{1,0:T(8,128)(2,1)}) %reduce-scatter.24.cloned.1.call-update) | async-done | bytes 655376 | tf_op jit(solution)/shard_map/reduce_scatter | solution.py:119
  703.5 51.6 %reduce-scatter.22.cloned.1.call-done = bf16[256,1280]{1,0:T(8,128)(2,1)} async-done(((bf16[1024,1280]{1,0:T(8,128)(2,1)}), bf16[256,1280]{1,0:T(8,128)(2,1)}) %reduce-scatter.22.cloned.1.call-update) | async-done | bytes 655376 | tf_op jit(solution)/shard_map/reduce_scatter | solution.py:110
  760.7 33.2 %all-gather.36.cloned.1.call-done = bf16[1024,768]{1,0:T(8,128)(2,1)} async-done(((bf16[256,768]{1,0:T(8,128)(2,1)}), bf16[1024,768]{1,0:T(8,128)(2,1)}) %all-gather.36.cloned.1.call-update) | async-done | bytes 1572880 | tf_op jit(solution)/shard_map/all_gather | solution.py:106
  839.2 10.6 all-gather.26.cloned.1.call-done
  919.3 9.8 copy.70
  947.4 9.8 fusion.38
  987.0 105.4 %all-reduce.30.cloned.1.call-done = f32[3,1280,384]{2,0,1:T(4,128)} async-done(((f32[3,1280,384]{2,0,1:T(4,128)}), f32[3,1280,384]{2,0,1:T(4,128)}) %all-reduce.30.cloned.1.call-update) | async-done | bytes 5898256
  1094.7 52.2 %reduce-scatter.26.cloned.1.call-done = bf16[256,1280]{1,0:T(8,128)(2,1)} async-done(((bf16[1024,1280]{1,0:T(8,128)(2,1)}), bf16[256,1280]{1,0:T(8,128)(2,1)}) %reduce-scatter.26.cloned.1.call-update) | async-done | bytes 655376 | tf_op jit(solution)/shard_map/reduce_scatter | solution.py:119
  1150.3 25.6 %all-reduce.25 = (f32[1280]{0:T(1024)S(1)}, f32[1280]{0:T(1024)S(1)}, f32[2,384]{1,0:T(2,128)}, f32[1280]{0:T(1024)S(1)}, f32[1280]{0:T(1024)S(1)}, /*index=5*/f...) all-reduce(f32[1280]{0:T(1024)S(1)} %get-tuple-element.86, ...), channel_id=8, replica_groups=mesh['dp'=8,'tensor'=4] {'dp'}, use_global_device_ids=true, to_apply=%region_20.21.clone | all-reduce | flops 15488 | bytes 123904
  1178.9 11.3 all-reduce.26
  1193.0 46.7 %reduce-scatter.42.cloned.1.call-done = f32[96,768]{1,0:T(8,128)} async-done(((f32[768,768]{1,0:T(8,128)}), f32[96,768]{1,0:T(8,128)}) %reduce-scatter.42.cloned.1.call-update) | async-done | bytes 294928 | tf_op jit(solution)/shard_map/reduce_scatter | solution.py:361
  1239.6 66.9 %reduce-scatter.32.cloned.1.call-done = f32[1280,160]{0,1:T(8,128)} async-done(((f32[1280,1280]{0,1:T(8,128)}), f32[1280,160]{0,1:T(8,128)}) %reduce-scatter.32.cloned.1.call-update) | async-done | bytes 819216 | tf_op jit(solution)/shard_map/reduce_scatter | solution.py:352
  1306.5 67.4 %reduce-scatter.30.cloned.1.call-done = f32[160,1280]{1,0:T(8,128)} async-done(((f32[1280,1280]{1,0:T(8,128)}), f32[160,1280]{1,0:T(8,128)}) %reduce-scatter.30.cloned.1.call-update) | async-done | bytes 819216 | tf_op jit(solution)/shard_map/reduce_scatter | solution.py:351
  1374.0 44.3 %reduce-scatter.28.cloned.1.call-done = f32[384,160]{0,1:T(8,128)} async-done(((f32[384,1280]{0,1:T(8,128)}), f32[384,160]{0,1:T(8,128)}) %reduce-scatter.28.cloned.1.call-update) | async-done | bytes 245776 | tf_op jit(solution)/shard_map/reduce_scatter | solution.py:350
  (541 shorter events, 320.4 us)
Async XLA Ops:
  7.3 85.9 %all-gather.28.cloned.1.call-start = ((), (), s32[]{:S(2)}) async-start(), calls=%async_computation.28 | async-start | bytes 1966080 | tf_op jit(solution)/shard_map/all_gather | solution.py:102
  51.0 92.6 %all-gather.16.cloned.1.call-start = ((), (), s32[]{:S(2)}) async-start(), calls=%async_computation.15 | async-start | bytes 3276800 | tf_op jit(solution)/shard_map/all_gather | solution.py:102
  53.9 121.9 %all-gather.18.cloned.1.call-start = ((), (), s32[]{:S(2)}) async-start(), calls=%async_computation.16 | async-start | bytes 3317760 | tf_op jit(solution)/shard_map/all_gather | solution.py:148
  54.7 158.6 %reduce-scatter.34.cloned.1.call-start = ((), (), s32[]{:S(2)}) async-start(), calls=%async_computation.29 | async-start | bytes 1966080 | tf_op jit(solution)/shard_map/reduce_scatter | solution.py:110
  107.5 159.1 %reduce-scatter.20.cloned.1.call-start = ((), (), s32[]{:S(2)}) async-start(), calls=%async_computation.17 | async-start | bytes 3276800 | tf_op jit(solution)/shard_map/reduce_scatter | solution.py:110
  208.4 83.7 %all-gather.32.cloned.1.call-start = ((), (), s32[]{:S(2)}) async-start(), calls=%async_computation.31 | async-start | bytes 1327104 | tf_op jit(solution)/shard_map/all_gather | solution.py:150
  209.0 122.3 %all-gather.30.cloned.1.call-start = ((), (), s32[]{:S(2)}) async-start(), calls=%async_computation.30 | async-start | bytes 1966080 | tf_op jit(solution)/shard_map/all_gather | solution.py:102
  217.8 138.4 %all-gather.34.cloned.1.call-start = ((), (), s32[]{:S(2)}) async-start(), calls=%async_computation.32 | async-start | bytes 1327104 | tf_op jit(solution)/shard_map/all_gather | solution.py:151
  218.6 176.3 %all-gather.40.cloned.1.call-start = ((), (), s32[]{:S(2)}) async-start(), calls=%async_computation.40 | async-start | bytes 1966080 | tf_op jit(solution)/shard_map/all_gather | solution.py:106
  219.3 209.1 %all-gather.22.cloned.1.call-start = ((), (), s32[]{:S(2)}) async-start(), calls=%async_computation.19 | async-start | bytes 3686400 | tf_op jit(solution)/shard_map/all_gather | solution.py:150
  219.9 265.5 %all-gather.20.cloned.1.call-start = ((), (), s32[]{:S(2)}) async-start(), calls=%async_computation.18 | async-start | bytes 3276800 | tf_op jit(solution)/shard_map/all_gather | solution.py:102
  271.8 268.6 %all-gather.38.cloned.1.call-start = ((), (), s32[]{:S(2)}) async-start(), calls=%async_computation.39 | async-start | bytes 3276800 | tf_op jit(solution)/shard_map/all_gather | solution.py:106
  272.4 301.6 %all-gather.24.cloned.1.call-start = ((), (), s32[]{:S(2)}) async-start(), calls=%async_computation.20 | async-start | bytes 3686400 | tf_op jit(solution)/shard_map/all_gather | solution.py:151
  273.1 338.3 %reduce-scatter.38.cloned.1.call-start = ((), (), s32[]{:S(2)}) async-start(), calls=%async_computation.34 | async-start | bytes 1966080 | tf_op jit(solution)/shard_map/reduce_scatter | solution.py:119
  405.0 242.9 %reduce-scatter.36.cloned.1.call-start = ((), (), s32[]{:S(2)}) async-start(), calls=%async_computation.33 | async-start | bytes 1966080 | tf_op jit(solution)/shard_map/reduce_scatter | solution.py:110
  410.5 290.6 %reduce-scatter.24.cloned.1.call-start = ((), (), s32[]{:S(2)}) async-start(), calls=%async_computation.22 | async-start | bytes 3276800 | tf_op jit(solution)/shard_map/reduce_scatter | solution.py:119
  591.1 164.0 %reduce-scatter.22.cloned.1.call-start = ((), (), s32[]{:S(2)}) async-start(), calls=%async_computation.21 | async-start | bytes 3276800 | tf_op jit(solution)/shard_map/reduce_scatter | solution.py:110
  601.0 193.0 %all-gather.36.cloned.1.call-start = ((), (), s32[]{:S(2)}) async-start(), calls=%async_computation.35 | async-start | bytes 1966080 | tf_op jit(solution)/shard_map/all_gather | solution.py:106
  652.4 197.4 %all-gather.26.cloned.1.call-start = ((), (), s32[]{:S(2)}) async-start(), calls=%async_computation.23 | async-start | bytes 3276800 | tf_op jit(solution)/shard_map/all_gather | solution.py:106
  760.6 211.8 %reduce-scatter.48.cloned.1.call-start = ((), (), s32[]{:S(2)}) async-start(), calls=%async_computation.42 | async-start | bytes 884736
  817.0 157.1 %reduce-scatter.46.cloned.1.call-start = ((), (), s32[]{:S(2)}) async-start(), calls=%async_computation.41 | async-start | bytes 2211840
  834.9 141.0 %reduce-scatter.40.cloned.1.call-start = ((), (), s32[]{:S(2)}) async-start(), calls=%async_computation.36 | async-start | bytes 1966080 | tf_op jit(solution)/shard_map/reduce_scatter | solution.py:119
  838.9 253.5 %all-reduce.30.cloned.1.call-start = ((), (), s32[]{:S(2)}) async-start(), calls=%async_computation.43 | async-start | bytes 15728640
  929.2 217.7 %reduce-scatter.26.cloned.1.call-start = ((), (), s32[]{:S(2)}) async-start(), calls=%async_computation.24 | async-start | bytes 3276800 | tf_op jit(solution)/shard_map/reduce_scatter | solution.py:119
  937.0 255.9 %reduce-scatter.44.cloned.1.call-start = ((), (), s32[]{:S(2)}) async-start(), calls=%async_computation.38 | async-start | bytes 2654208 | tf_op jit(solution)/shard_map/reduce_scatter | solution.py:362
  942.4 297.3 %reduce-scatter.42.cloned.1.call-start = ((), (), s32[]{:S(2)}) async-start(), calls=%async_computation.37 | async-start | bytes 2654208 | tf_op jit(solution)/shard_map/reduce_scatter | solution.py:361
  947.3 359.2 %reduce-scatter.32.cloned.1.call-start = ((), (), s32[]{:S(2)}) async-start(), calls=%async_computation.27 | async-start | bytes 7372800 | tf_op jit(solution)/shard_map/reduce_scatter | solution.py:352
  957.2 416.7 %reduce-scatter.30.cloned.1.call-start = ((), (), s32[]{:S(2)}) async-start(), calls=%async_computation.26 | async-start | bytes 7372800 | tf_op jit(solution)/shard_map/reduce_scatter | solution.py:351
  966.2 452.1 %reduce-scatter.28.cloned.1.call-start = ((), (), s32[]{:S(2)}) async-start(), calls=%async_computation.25 | async-start | bytes 2211840 | tf_op jit(solution)/shard_map/reduce_scatter | solution.py:350
  987.0 203.3 %copy-start.15 = (f32[256,1280]{1,0:T(8,128)S(1)}, f32[256,1280]{1,0:T(8,128)}, u32[]{:S(2)}) copy-start(f32[256,1280]{1,0:T(8,128)} %copy-done.14) | copy-start | bytes 3932164
  987.0 203.3 %copy-start.24 = (bf16[1,256,1280]{2,1,0:T(8,128)(2,1)S(1)}, bf16[1,256,1280]{2,1,0:T(8,128)(2,1)}, u32[]{:S(2)}) copy-start(bf16[1,256,1280]{2,1,0:T(8,128)(2,1)} %param.31) | copy-start | bytes 1966084
  987.0 203.3 %copy-start.87 = (f32[256]{0:T(256)S(1)}, f32[256]{0:T(256)}, u32[]{:S(2)}) copy-start(f32[256]{0:T(256)} %copy-done.86) | copy-start | bytes 3076
  (132 other events, 3972.0 us)
Sparse Core Ops, SparseCore 0:
  51.1 36.5 all-gather.27
  89.9 53.6 all-gather.15
  145.5 30.2 all-gather.17
  178.0 35.2 reduce-scatter.33
  215.5 51.0 reduce-scatter.19
  268.3 23.7 all-gather.31
  294.2 37.0 all-gather.29
  333.2 22.9 all-gather.33
  357.8 37.0 all-gather.39
  396.6 31.7 all-gather.21
  430.5 54.7 all-gather.19
  486.8 53.5 all-gather.37
  542.3 31.6 all-gather.23
  576.1 35.2 reduce-scatter.37
  613.6 34.2 reduce-scatter.35
  650.1 51.0 reduce-scatter.23
  703.3 51.7 reduce-scatter.21
  757.2 36.7 all-gather.35
  796.1 53.6 all-gather.25
  852.8 33.8 reduce-scatter.47
  890.2 40.2 reduce-scatter.45
  932.9 35.2 reduce-scatter.39
  971.9 120.4 all-reduce.29
  1094.6 52.2 reduce-scatter.25
  1150.8 42.1 reduce-scatter.43
  1197.1 42.4 reduce-scatter.41
  1243.5 62.9 reduce-scatter.31
  1311.0 62.9 reduce-scatter.29
  1378.0 40.2 reduce-scatter.27
where the time goes:
time: 1430 us
  waiting for transfers between devices  967 us (68%)
  matrix products  200 us (14%)
  blocking collectives  96.7 us (7%)
  other arithmetic  80.5 us (6%)
  local copies, waits for them, and re-layouts  57.9 us (4%)
  between operations  19.8 us (1%)
    reduce_scatter x4, waiting for transfers between devices, sum_rows(): lax.psum_scatter(jnp.dot(left_rows, right_weight, preferred_element_type=...  137 us
    all_gather x4, waiting for transfers between devices, gather_rows(): return lax.all_gather(normed, 'tensor', axis=0, tiled=True)  132 us
    all_gather x4, waiting for transfers between devices, gather_grads(): return lax.all_gather(branch_grad, 'tensor', axis=0, tiled=True)  129 us
    reduce_scatter x4, waiting for transfers between devices, back_rows(): lax.psum_scatter(jnp.einsum('sle,sde->ld', grad_stack, weight_stack, pref...  111 us
    unnamed x32, waiting for transfers between devices  110 us
    reduce_scatter x1, waiting for transfers between devices, on_device(): lax.psum_scatter(teach_parts[2], 'dp', scatter_dimension=0, tiled=True)  67.4 us
    reduce_scatter x1, waiting for transfers between devices, on_device(): lax.psum_scatter(teach_parts[3], 'dp', scatter_dimension=1, tiled=True)  66.9 us
    all_gather x2, waiting for transfers between devices, run_block(): lax.all_gather(proj_weight, 'dp', axis=1, tiled=True)  53.6 us
  transfers between devices with their start and end apart: 29, of which 25 were waited for; matrix products, arithmetic and copies ran while one was open for 22% of the time, Pallas kernels for 0%

commit v1 on v0

--- a/solution.py
+++ b/solution.py
@@ -103,7 +103,22 @@
 
 
 def gather_grads(branch_grad):
-    return lax.all_gather(branch_grad, "tensor", axis=0, tiled=True)
+
+    def shelves_wait(field, out_dim):
+        tall, answer = (lax.axis_size("tensor"), lax.axis_index("tensor"))
+        b_next, res = (field, 1)
+        while res < tall:
+            by_rank = []
+            for no in [*range(tall)]:
+                by_rank.append((no, no ^ res))
+            t_next = lax.ppermute(b_next, axis_name="tensor", perm=by_rank)
+            o_now = jnp.concatenate([b_next, t_next], axis=out_dim)
+            y2 = jnp.concatenate([t_next, b_next], axis=out_dim)
+            b_next = jnp.where(answer & res == 0, o_now, y2)
+            res = 2 * res
+        return b_next
+
+    return shelves_wait(branch_grad, 0)
 
 
 def sum_rows(left_rows, right_weight):

time: 1430 us -> 1360 us (0.951)
  waiting for transfers between devices: 967 us -> 872 us
    ppermute x0 -> x8, waiting for transfers between devices: none -> 177 us  [shelves_wait(): t_next = lax.ppermute(b_next, axis_name='tensor', perm=by_rank)]
    all_gather x4 -> x0, waiting for transfers between devices: 129 us -> none  [gather_grads(): return lax.all_gather(branch_grad, 'tensor', axis=0, tiled=True)]
    unnamed x32 -> x28, waiting for transfers between devices: 110 us -> 52.8 us
    reduce_scatter x4, waiting for transfers between devices: 137 us -> 86.2 us  [sum_rows(): lax.psum_scatter(jnp.dot(left_rows, right_weight, preferred_element_type=...]
    all_gather x4, waiting for transfers between devices: 132 us -> 175 us  [gather_rows(): return lax.all_gather(normed, 'tensor', axis=0, tiled=True)]
    reduce_scatter x4, waiting for transfers between devices: 111 us -> 70.3 us  [back_rows(): lax.psum_scatter(jnp.einsum('sle,sde->ld', grad_stack, weight_stack, pref...]
    all_gather x2, waiting for transfers between devices: 36 us -> 6.86 us  [run_block(): lax.all_gather(fc_weight, 'dp', axis=0, tiled=True)]
    unnamed x316 -> x298, local copies, waits for them, and re-layouts: 42 us -> 44.3 us
  transfers between devices with their start and end apart: 29 -> 33, of which waited for: 25 -> 24; matrix products, arithmetic and copies ran while one was open for 22% -> 24% of each run, Pallas kernels for 0% -> 0%
where the time goes in v1:
time: 1360 us; the launch traced here: 1350 us
  waiting for transfers between devices  872 us (64%)
  matrix products  203 us (15%)
  blocking collectives  96.7 us (7%)
  other arithmetic  89.2 us (7%)
  local copies, waits for them, and re-layouts  60.4 us (4%)
  between operations  19.4 us (1%)
    ppermute x8, waiting for transfers between devices, shelves_wait(): t_next = lax.ppermute(b_next, axis_name='tensor', perm=by_rank)  177 us
    all_gather x4, waiting for transfers between devices, gather_rows(): return lax.all_gather(normed, 'tensor', axis=0, tiled=True)  175 us
    reduce_scatter x4, waiting for transfers between devices, sum_rows(): lax.psum_scatter(jnp.dot(left_rows, right_weight, preferred_element_type=...  86.2 us
    reduce_scatter x4, waiting for transfers between devices, back_rows(): lax.psum_scatter(jnp.einsum('sle,sde->ld', grad_stack, weight_stack, pref...  70.3 us
    reduce_scatter x1, waiting for transfers between devices, on_device(): lax.psum_scatter(teach_parts[2], 'dp', scatter_dimension=0, tiled=True)  67.3 us
    reduce_scatter x1, waiting for transfers between devices, on_device(): lax.psum_scatter(teach_parts[3], 'dp', scatter_dimension=1, tiled=True)  67.1 us
    unnamed x28, waiting for transfers between devices  52.8 us
    unnamed x2, blocking collectives  52 us
  transfers between devices with their start and end apart: 33, of which 24 were waited for; matrix products, arithmetic and copies ran while one was open for 24% of the time, Pallas kernels for 0%

profile of v1, /device:TPU:0, one launch (start us, length us, event | category | flops | bytes accessed | tf_op | source)
XLA Modules:
  0.0 1352.5 jit_solution(13634727479654542177)
XLA Ops:
  23.1 26.5 %all-reduce.27 = (bf16[1280]{0:T(1024)(128)(2,1)S(1)}, bf16[1280]{0:T(1024)(128)(2,1)S(1)}, bf16[1280]{0:T(1024)(128)(2,1)S(1)}, bf16[1280]{0:T(1024)(128)(2,1)S...) all-reduce(bf16[1280]{0:T(1024)(128)(2,1)S(1)} %dynamic-update-slic, ...), channel_id=1, replica_groups=mesh['dp'=8,'tensor'=4] {'dp'}, use_global_device_ids=true, to_apply=%add.4 | all-reduce | flops 12288 | bytes 49152
  58.5 10.9 all_gather.76
  69.5 13.4 all_gather.87
  109.6 35.0 %all-gather.10.cloned.1.call-done = bf16[1024,1280]{1,0:T(8,128)(2,1)} async-done(((bf16[256,1280]{1,0:T(8,128)(2,1)}), bf16[1024,1280]{1,0:T(8,128)(2,1)}) %all-gather.10.cloned.1.call-update) | async-done | bytes 2621456 | tf_op jit(solution)/shard_map/all_gather | solution.py:102
  144.7 32.2 %all-gather.12.cloned.1.call-done = bf16[3,1280,384]{2,1,0:T(8,128)(2,1)} async-done(((bf16[3,160,384]{2,1,0:T(8,128)(2,1)}), bf16[3,1280,384]{2,1,0:T(8,128)(2,1)}) %all-gather.12.cloned.1.call-update) | async-done | bytes 2949136 | tf_op jit(solution)/shard_map/all_gather | solution.py:163
  220.4 47.2 %reduce-scatter.20.cloned.1.call-done = bf16[256,1280]{1,0:T(8,128)(2,1)} async-done(((bf16[1024,1280]{1,0:T(8,128)(2,1)}), bf16[256,1280]{1,0:T(8,128)(2,1)}) %reduce-scatter.20.cloned.1.call-update) | async-done | bytes 655376 | tf_op jit(solution)/shard_map/reduce_scatter | solution.py:125
  273.5 10.0 collective-permute-done.4
  293.1 52.3 %all-gather.22.cloned.1.call-done = bf16[1024,768]{1,0:T(8,128)(2,1)} async-done(((bf16[256,768]{1,0:T(8,128)(2,1)}), bf16[1024,768]{1,0:T(8,128)(2,1)}) %all-gather.22.cloned.1.call-update) | async-done | bytes 1572880 | tf_op jit(solution)/shard_map/all_gather | solution.py:102
  350.2 20.0 %all-gather.26.cloned.1.call-done = bf16[768,768]{0,1:T(8,128)(2,1)} async-done(((bf16[768,96]{0,1:T(8,128)(2,1)}), bf16[768,768]{0,1:T(8,128)(2,1)}) %all-gather.26.cloned.1.call-update) | async-done | bytes 1179664 | tf_op jit(solution)/shard_map/all_gather | solution.py:166
  382.2 15.4 %collective-permute-done = bf16[256,1280]{1,0:T(8,128)(2,1)S(1)} collective-permute-done((bf16[256,1280]{1,0:T(8,128)(2,1)S(1)}, bf16[256,1280]{1,0:T(8,128)(2,1)S(1)}, u32[]{:S(2)}, u32[]{:S(2)}) %collective-permute-start) | collective-permute-done | bytes 655392 | tf_op jit(solution)/shard_map/ppermute | solution.py:114
  407.5 87.8 %all-gather.14.cloned.1.call-done = bf16[1024,1280]{1,0:T(8,128)(2,1)} async-done(((bf16[256,1280]{1,0:T(8,128)(2,1)}), bf16[1024,1280]{1,0:T(8,128)(2,1)}) %all-gather.14.cloned.1.call-update) | async-done | bytes 2621456 | tf_op jit(solution)/shard_map/all_gather | solution.py:102
  503.9 25.2 %all-gather.18.cloned.1.call-done = bf16[1280,1280]{0,1:T(8,128)(2,1)} async-done(((bf16[1280,160]{0,1:T(8,128)(2,1)}), bf16[1280,1280]{0,1:T(8,128)(2,1)}) %all-gather.18.cloned.1.call-update) | async-done | bytes 3276816 | tf_op jit(solution)/shard_map/all_gather | solution.py:166
  529.1 12.3 convert_reduce_fusion.1
  548.4 18.2 %reduce-scatter.38.cloned.1.call-done = bf16[256,768]{1,0:T(8,128)(2,1)} async-done(((bf16[1024,768]{1,0:T(8,128)(2,1)}), bf16[256,768]{1,0:T(8,128)(2,1)}) %reduce-scatter.38.cloned.1.call-update) | async-done | bytes 393232 | tf_op jit(solution)/shard_map/reduce_scatter | solution.py:134
  568.6 34.6 %reduce-scatter.36.cloned.1.call-done = bf16[256,768]{1,0:T(8,128)(2,1)} async-done(((bf16[1024,768]{1,0:T(8,128)(2,1)}), bf16[256,768]{1,0:T(8,128)(2,1)}) %reduce-scatter.36.cloned.1.call-update) | async-done | bytes 393232 | tf_op jit(solution)/shard_map/reduce_scatter | solution.py:125
  605.5 9.9 convolution_convert_fusion.2
  616.1 27.3 %collective-permute-done.6 = bf16[256,768]{1,0:T(8,128)(2,1)S(1)} collective-permute-done((bf16[256,768]{1,0:T(8,128)(2,1)S(1)}, bf16[256,768]{1,0:T(8,128)(2,1)S(1)}, u32[]{:S(2)}, u32[]{:S(2)}) %collective-permute-start.6) | collective-permute-done | bytes 393248 | tf_op jit(solution)/shard_map/ppermute | solution.py:114
  643.9 52.3 %collective-permute-done.7 = bf16[512,768]{1,0:T(8,128)(2,1)S(1)} collective-permute-done((bf16[512,768]{1,0:T(8,128)(2,1)S(1)}, bf16[512,768]{1,0:T(8,128)(2,1)S(1)}, u32[]{:S(2)}, u32[]{:S(2)}) %collective-permute-start.7) | collective-permute-done | bytes 786464 | tf_op jit(solution)/shard_map/ppermute | solution.py:114
  740.3 16.2 %collective-permute-done.2 = bf16[256,1280]{1,0:T(8,128)(2,1)S(1)} collective-permute-done((bf16[256,1280]{1,0:T(8,128)(2,1)S(1)}, bf16[256,1280]{1,0:T(8,128)(2,1)S(1)}, u32[]{:S(2)}, u32[]{:S(2)}) %collective-permute-start.2) | collective-permute-done | bytes 655392 | tf_op jit(solution)/shard_map/ppermute | solution.py:114
  761.7 55.5 %collective-permute-done.3 = bf16[512,1280]{1,0:T(8,128)(2,1)} collective-permute-done((bf16[512,1280]{1,0:T(8,128)(2,1)}, bf16[512,1280]{1,0:T(8,128)(2,1)}, u32[]{:S(2)}, u32[]{:S(2)}) %collective-permute-start.3) | collective-permute-done | bytes 1310752 | tf_op jit(solution)/shard_map/ppermute | solution.py:114
  828.0 9.3 multiply_reduce_fusion
  847.1 9.8 multiply_convert_fusion.1
  890.1 9.8 copy.70
  918.6 11.0 fusion.145
  970.5 49.2 %all-reduce.30.cloned.1.call-done = f32[3,1280,384]{2,0,1:T(4,128)} async-done(((f32[3,1280,384]{2,0,1:T(4,128)}), f32[3,1280,384]{2,0,1:T(4,128)}) %all-reduce.30.cloned.1.call-update) | async-done | bytes 5898256
  1022.0 52.1 %reduce-scatter.26.cloned.1.call-done = bf16[256,1280]{1,0:T(8,128)(2,1)} async-done(((bf16[1024,1280]{1,0:T(8,128)(2,1)}), bf16[256,1280]{1,0:T(8,128)(2,1)}) %reduce-scatter.26.cloned.1.call-update) | async-done | bytes 655376 | tf_op jit(solution)/shard_map/reduce_scatter | solution.py:134
  1077.7 25.6 %all-reduce.25 = (f32[1280]{0:T(1024)S(1)}, f32[1280]{0:T(1024)S(1)}, f32[2,384]{1,0:T(2,128)}, f32[1280]{0:T(1024)S(1)}, f32[1280]{0:T(1024)S(1)}, /*index=5*/f...) all-reduce(f32[1280]{0:T(1024)S(1)} %get-tuple-element.86, ...), channel_id=6, replica_groups=mesh['dp'=8,'tensor'=4] {'dp'}, use_global_device_ids=true, to_apply=%region_20.21.clone | all-reduce | flops 15488 | bytes 123904
  1106.3 11.3 all-reduce.26
  1120.3 46.8 %reduce-scatter.42.cloned.1.call-done = f32[96,768]{1,0:T(8,128)} async-done(((f32[768,768]{1,0:T(8,128)}), f32[96,768]{1,0:T(8,128)}) %reduce-scatter.42.cloned.1.call-update) | async-done | bytes 294928 | tf_op jit(solution)/shard_map/reduce_scatter | solution.py:376
  1167.1 67.1 %reduce-scatter.32.cloned.1.call-done = f32[1280,160]{0,1:T(8,128)} async-done(((f32[1280,1280]{0,1:T(8,128)}), f32[1280,160]{0,1:T(8,128)}) %reduce-scatter.32.cloned.1.call-update) | async-done | bytes 819216 | tf_op jit(solution)/shard_map/reduce_scatter | solution.py:367
  1234.2 67.3 %reduce-scatter.30.cloned.1.call-done = f32[160,1280]{1,0:T(8,128)} async-done(((f32[1280,1280]{1,0:T(8,128)}), f32[160,1280]{1,0:T(8,128)}) %reduce-scatter.30.cloned.1.call-update) | async-done | bytes 819216 | tf_op jit(solution)/shard_map/reduce_scatter | solution.py:366
  1301.5 44.3 %reduce-scatter.28.cloned.1.call-done = f32[384,160]{0,1:T(8,128)} async-done(((f32[384,1280]{0,1:T(8,128)}), f32[384,160]{0,1:T(8,128)}) %reduce-scatter.28.cloned.1.call-update) | async-done | bytes 245776 | tf_op jit(solution)/shard_map/reduce_scatter | solution.py:365
  (531 shorter events, 327.1 us)
Async XLA Ops:
  7.3 87.0 %all-gather.20.cloned.1.call-start = ((), (), s32[]{:S(2)}) async-start(), calls=%async_computation.27 | async-start | bytes 1966080 | tf_op jit(solution)/shard_map/all_gather | solution.py:102
  52.2 92.5 %all-gather.10.cloned.1.call-start = ((), (), s32[]{:S(2)}) async-start(), calls=%async_computation.15 | async-start | bytes 3276800 | tf_op jit(solution)/shard_map/all_gather | solution.py:102
  56.2 120.7 %all-gather.12.cloned.1.call-start = ((), (), s32[]{:S(2)}) async-start(), calls=%async_computation.16 | async-start | bytes 3317760 | tf_op jit(solution)/shard_map/all_gather | solution.py:163
  56.9 157.4 %reduce-scatter.34.cloned.1.call-start = ((), (), s32[]{:S(2)}) async-start(), calls=%async_computation.28 | async-start | bytes 1966080 | tf_op jit(solution)/shard_map/reduce_scatter | solution.py:125
  109.0 158.6 %reduce-scatter.20.cloned.1.call-start = ((), (), s32[]{:S(2)}) async-start(), calls=%async_computation.17 | async-start | bytes 3276800 | tf_op jit(solution)/shard_map/reduce_scatter | solution.py:125
  209.3 83.9 %all-gather.24.cloned.1.call-start = ((), (), s32[]{:S(2)}) async-start(), calls=%async_computation.30 | async-start | bytes 1327104 | tf_op jit(solution)/shard_map/all_gather | solution.py:165
  209.8 135.6 %all-gather.22.cloned.1.call-start = ((), (), s32[]{:S(2)}) async-start(), calls=%async_computation.29 | async-start | bytes 1966080 | tf_op jit(solution)/shard_map/all_gather | solution.py:102
  218.8 151.4 %all-gather.26.cloned.1.call-start = ((), (), s32[]{:S(2)}) async-start(), calls=%async_computation.31 | async-start | bytes 1327104 | tf_op jit(solution)/shard_map/all_gather | solution.py:166
  219.6 187.9 %all-gather.16.cloned.1.call-start = ((), (), s32[]{:S(2)}) async-start(), calls=%async_computation.19 | async-start | bytes 3686400 | tf_op jit(solution)/shard_map/all_gather | solution.py:165
  220.3 275.0 %all-gather.14.cloned.1.call-start = ((), (), s32[]{:S(2)}) async-start(), calls=%async_computation.18 | async-start | bytes 3276800 | tf_op jit(solution)/shard_map/all_gather | solution.py:102
  271.8 257.3 %all-gather.18.cloned.1.call-start = ((), (), s32[]{:S(2)}) async-start(), calls=%async_computation.20 | async-start | bytes 3686400 | tf_op jit(solution)/shard_map/all_gather | solution.py:166
  272.6 294.0 %reduce-scatter.38.cloned.1.call-start = ((), (), s32[]{:S(2)}) async-start(), calls=%async_computation.33 | async-start | bytes 1966080 | tf_op jit(solution)/shard_map/reduce_scatter | solution.py:134
  283.9 66.3 %collective-permute-start.5 = (bf16[512,768]{1,0:T(8,128)(2,1)S(1)}, bf16[512,768]{1,0:T(8,128)(2,1)}, u32[]{:S(2)}, u32[]{:S(2)}) collective-permute-start(bf16[512,768]{1,0:T(8,128)(2,1)S(1)} %maximum_select_fusion.6), channel_id=1, source_target_pairs={{0,2},{1,3},{2,0},{3,1},{4,6},{5,7},{6,4},{7,5},{8,10},{9,11},{10,... | collective-permute-start | bytes 2359304 | tf_op jit(solution)/shard_map/ppermute | solution.py:114
  380.6 222.6 %reduce-scatter.36.cloned.1.call-start = ((), (), s32[]{:S(2)}) async-start(), calls=%async_computation.32 | async-start | bytes 1966080 | tf_op jit(solution)/shard_map/reduce_scatter | solution.py:125
  380.6 17.0 %collective-permute-start = (bf16[256,1280]{1,0:T(8,128)(2,1)S(1)}, bf16[256,1280]{1,0:T(8,128)(2,1)S(1)}, u32[]{:S(2)}, u32[]{:S(2)}) collective-permute-start(bf16[256,1280]{1,0:T(8,128)(2,1)S(1)} %bitcast.310), channel_id=1, source_target_pairs={{0,1},{1,0},{2,3},{3,2},{4,5},{5,4},{6,7},{7,6},{8,9},{9,8},{10,11... | collective-permute-start | bytes 1966088 | tf_op jit(solution)/shard_map/ppermute | solution.py:114
  399.2 104.7 %collective-permute-start.1 = (bf16[512,1280]{1,0:T(8,128)(2,1)}, bf16[512,1280]{1,0:T(8,128)(2,1)}, u32[]{:S(2)}, u32[]{:S(2)}) collective-permute-start(bf16[512,1280]{1,0:T(8,128)(2,1)} %maximum_select_fusion.4), channel_id=1, source_target_pairs={{0,2},{1,3},{2,0},{3,1},{4,6},{5,7},{6,4},{7,5},{8,10},{9,11},{10,... | collective-permute-start | bytes 3932168 | tf_op jit(solution)/shard_map/ppermute | solution.py:114
  407.2 327.1 %reduce-scatter.24.cloned.1.call-start = ((), (), s32[]{:S(2)}) async-start(), calls=%async_computation.22 | async-start | bytes 3276800 | tf_op jit(solution)/shard_map/reduce_scatter | solution.py:134
  547.9 188.9 %reduce-scatter.22.cloned.1.call-start = ((), (), s32[]{:S(2)}) async-start(), calls=%async_computation.21 | async-start | bytes 3276800 | tf_op jit(solution)/shard_map/reduce_scatter | solution.py:125
  615.4 333.9 %reduce-scatter.48.cloned.1.call-start = ((), (), s32[]{:S(2)}) async-start(), calls=%async_computation.38 | async-start | bytes 884736
  615.7 27.7 %collective-permute-start.6 = (bf16[256,768]{1,0:T(8,128)(2,1)S(1)}, bf16[256,768]{1,0:T(8,128)(2,1)S(1)}, u32[]{:S(2)}, u32[]{:S(2)}) collective-permute-start(bf16[256,768]{1,0:T(8,128)(2,1)S(1)} %fusion.119), channel_id=1, source_target_pairs={{0,1},{1,0},{2,3},{3,2},{4,5},{5,4},{6,7},{7,6},{8,9},{9,8},{10,11... | collective-permute-start | bytes 1179656 | tf_op jit(solution)/shard_map/ppermute | solution.py:114
  643.8 52.4 %collective-permute-start.7 = (bf16[512,768]{1,0:T(8,128)(2,1)S(1)}, bf16[512,768]{1,0:T(8,128)(2,1)S(1)}, u32[]{:S(2)}, u32[]{:S(2)}) collective-permute-start(bf16[512,768]{1,0:T(8,128)(2,1)S(1)} %maximum_select_fusion.7), channel_id=1, source_target_pairs={{0,2},{1,3},{2,0},{3,1},{4,6},{5,7},{6,4},{7,5},{8,10},{9,11},{10,... | collective-permute-start | bytes 2359304 | tf_op jit(solution)/shard_map/ppermute | solution.py:114
  715.6 235.3 %reduce-scatter.46.cloned.1.call-start = ((), (), s32[]{:S(2)}) async-start(), calls=%async_computation.37 | async-start | bytes 2211840
  734.3 218.6 %reduce-scatter.40.cloned.1.call-start = ((), (), s32[]{:S(2)}) async-start(), calls=%async_computation.34 | async-start | bytes 1966080 | tf_op jit(solution)/shard_map/reduce_scatter | solution.py:134
  739.8 16.7 %collective-permute-start.2 = (bf16[256,1280]{1,0:T(8,128)(2,1)S(1)}, bf16[256,1280]{1,0:T(8,128)(2,1)S(1)}, u32[]{:S(2)}, u32[]{:S(2)}) collective-permute-start(bf16[256,1280]{1,0:T(8,128)(2,1)S(1)} %fusion.104), channel_id=1, source_target_pairs={{0,1},{1,0},{2,3},{3,2},{4,5},{5,4},{6,7},{7,6},{8,9},{9,8},{10,11... | collective-permute-start | bytes 1966088 | tf_op jit(solution)/shard_map/ppermute | solution.py:114
  758.2 59.1 %collective-permute-start.3 = (bf16[512,1280]{1,0:T(8,128)(2,1)}, bf16[512,1280]{1,0:T(8,128)(2,1)}, u32[]{:S(2)}, u32[]{:S(2)}) collective-permute-start(bf16[512,1280]{1,0:T(8,128)(2,1)} %maximum_select_fusion.5), channel_id=1, source_target_pairs={{0,2},{1,3},{2,0},{3,1},{4,6},{5,7},{6,4},{7,5},{8,10},{9,11},{10,... | collective-permute-start | bytes 3932168 | tf_op jit(solution)/shard_map/ppermute | solution.py:114
  761.5 258.2 %all-reduce.30.cloned.1.call-start = ((), (), s32[]{:S(2)}) async-start(), calls=%async_computation.39 | async-start | bytes 15728640
  899.9 174.3 %reduce-scatter.26.cloned.1.call-start = ((), (), s32[]{:S(2)}) async-start(), calls=%async_computation.23 | async-start | bytes 3276800 | tf_op jit(solution)/shard_map/reduce_scatter | solution.py:134
  907.7 212.6 %reduce-scatter.44.cloned.1.call-start = ((), (), s32[]{:S(2)}) async-start(), calls=%async_computation.36 | async-start | bytes 2654208 | tf_op jit(solution)/shard_map/reduce_scatter | solution.py:377
  913.8 253.4 %reduce-scatter.42.cloned.1.call-start = ((), (), s32[]{:S(2)}) async-start(), calls=%async_computation.35 | async-start | bytes 2654208 | tf_op jit(solution)/shard_map/reduce_scatter | solution.py:376
  918.5 315.6 %reduce-scatter.32.cloned.1.call-start = ((), (), s32[]{:S(2)}) async-start(), calls=%async_computation.26 | async-start | bytes 7372800 | tf_op jit(solution)/shard_map/reduce_scatter | solution.py:367
  929.6 371.8 %reduce-scatter.30.cloned.1.call-start = ((), (), s32[]{:S(2)}) async-start(), calls=%async_computation.25 | async-start | bytes 7372800 | tf_op jit(solution)/shard_map/reduce_scatter | solution.py:366
  938.7 407.0 %reduce-scatter.28.cloned.1.call-start = ((), (), s32[]{:S(2)}) async-start(), calls=%async_computation.24 | async-start | bytes 2211840 | tf_op jit(solution)/shard_map/reduce_scatter | solution.py:365
  (127 other events, 3535.1 us)
Sparse Core Ops, SparseCore 0:
  52.3 36.4 all-gather.19
  91.0 53.6 all-gather.9
  146.6 30.2 all-gather.11
  179.0 35.2 reduce-scatter.33
  216.5 51.0 reduce-scatter.19
  269.4 23.7 all-gather.23
  295.2 50.0 all-gather.21
  347.3 22.9 all-gather.25
  372.2 32.8 all-gather.15
  407.0 88.2 all-gather.13
  497.2 31.8 all-gather.17
  531.2 35.2 reduce-scatter.37
  568.9 34.2 reduce-scatter.35
  605.3 75.4 reduce-scatter.23
  683.0 53.5 reduce-scatter.21
  739.6 33.3 reduce-scatter.47
  776.2 40.2 reduce-scatter.45
  818.8 35.2 reduce-scatter.39
  900.0 119.6 all-reduce.29
  1021.9 52.2 reduce-scatter.25
  1078.1 42.1 reduce-scatter.43
  1124.6 42.4 reduce-scatter.41
  1171.1 63.0 reduce-scatter.31
  1238.5 62.9 reduce-scatter.29
  1305.4 40.2 reduce-scatter.27
